TPU v7x, 32 devices: a whole 2x2x4 slice. The times are simulated.
32 devices in a mesh: parts: 2 (over y), tmpl: 4 (over z), sta: 4 (over x, core).
Axes of the slice: x: 2, y: 2, z: 4, core: 2. Of those that a mesh axis runs over, the one named last changes fastest.
Arguments:
- data: float32 [64, 3, 1280], P(('parts', 'sta'), None, 'tmpl'), parts along dimension 0, as said below
- templates: bfloat16 [32, 3, 16, 256], P('sta', None, 'tmpl'), as said below
- starts: int32 [32, 3, 16], P('sta', None, 'tmpl'), may hold values from 0 to 512
Outputs:
- network: float32 [32, 512], P(('parts', 'tmpl'), 'sta'), parts along dimension 0
There are 2 independent parts, one for each index of `parts`. A program takes and returns all parts, laid end to end along the dimension named above; an argument that names none is the same for every part. Nothing has to cross between parts.
Inputs may be any that keep to these rules, and one draw needn't show every extreme that they name: `data`: finite samples. `templates`: finite samples.
All inputs are finite; a program needn't handle non-finite values.
Results may differ from a plain program's by a relative error of at most 0.0029.
Values sent between devices are 32-bit elements; how exact they have to be, the bound alone decides.
A program may use at most 64 MiB of HBM per device.

v0:
```python
import jax
import jax.numpy as jnp
from jax import lax
from jax.sharding import PartitionSpec as P

TLEN = 256
MAXSHIFT = 512
LAGS = 512
EPS = 1e-06


def window_energy(trace):
    extent = LAGS + MAXSHIFT
    squares = trace * trace
    running = jnp.concatenate([jnp.zeros_like(squares[:, :1]), jnp.cumsum(squares, axis=1)], axis=1)
    return running[:, TLEN : TLEN + extent] - running[:, :extent]


def take_window(row, offset):
    return lax.dynamic_slice_in_dim(row, offset, LAGS, 0)


def local_term(whole, templates, starts):
    extent = LAGS + MAXSHIFT
    stations, channels, samples = whole.shape
    per_group = templates.shape[2]
    groups = stations * channels
    lowered = whole.astype(jnp.bfloat16).reshape(1, groups, samples)
    kernel = templates.reshape(groups * per_group, 1, templates.shape[-1])
    raw = lax.conv_general_dilated(
        lowered,
        kernel,
        (1,),
        "VALID",
        dimension_numbers=("NCH", "OIH", "NCH"),
        feature_group_count=groups,
        preferred_element_type=jnp.float32,
    )[0]
    raw = raw[:, :extent]
    energy = window_energy(whole.reshape(groups, samples))
    energy_rows = jnp.repeat(energy, per_group, axis=0)
    tnorm = jnp.sum(jnp.square(templates.astype(jnp.float32)), axis=-1).reshape(-1)
    offsets = starts.reshape(-1)
    slicer = jax.vmap(take_window)
    aligned = slicer(raw, offsets)
    local = slicer(energy_rows, offsets)
    scale = TLEN * jnp.sqrt((tnorm[:, None] / TLEN + EPS) * (local / TLEN + EPS))
    return jnp.sum((aligned / scale).reshape(groups, per_group, LAGS), axis=0)


def shards(data, templates, starts):
    whole = lax.all_gather(data, "tmpl", axis=2, tiled=True)
    partial_value = local_term(whole, templates, starts)
    summed = lax.psum(partial_value, "sta")
    width = LAGS // lax.axis_size("sta")
    return lax.dynamic_slice_in_dim(summed, lax.axis_index("sta") * width, width, 1)


def solution(mesh):
    return jax.shard_map(
        shards,
        mesh=mesh,
        in_specs=(
            P(("parts", "sta"), None, "tmpl"),
            P("sta", None, "tmpl", None),
            P("sta", None, "tmpl"),
        ),
        out_specs=P(("parts", "tmpl"), "sta"),
        check_vma=False,
    )
```

profile of v0, /device:TPU:0, one launch (start us, length us, event | category | flops | bytes accessed | tf_op | source)
XLA Modules:
  0.0 490.5 jit_solution(16499657202032533554)
XLA Ops:
  1.0 47.9 %all_gather.3 = f32[8,3,1280]{0,1,2:T(4,128)S(1)} all-gather(f32[8,3,320]{0,1,2:T(4,128)S(1)} %copy.29), channel_id=1, replica_groups=mesh['parts'=2,'tmpl'=4,'sta'=4] {'tmpl'}, dimensions={2}, use_global_device_ids=true | all-gather | bytes 153600 | tf_op jit(solution)/shard_map/all_gather | solution.py:52
  49.9 6.8 %reduce-window.6 = f32[24,10,128]{2,1,0:T(8,128)S(1)} reduce-window(f32[24,10,128]{2,1,0:T(8,128)S(1)} %mul.25, f32[]{:T(128)} %constant.9.clone.1), window={size=1x1x128 pad=0_0x0_0x127_0}, to_apply=%region_1.2 | reduce-window | flops 3901440 | bytes 245764 | tf_op jit(solution)/shard_map/reduce-window
  58.0 197.6 %while.3 = (s32[]{:T(128)}, f32[96,1024]{1,0:T(8,128)S(1)}, s32[96,2]{0,1:T(2,128)S(1)}, f32[96,512]{1,0:T(8,128)S(1)}, s32[]{:T(128)}, /*index=5*/s32[]{:T(128)}) while((s32[]{:T(128)}, f32[96,1024]{1,0:T(8,128)S(1)}, s32[96,2]{0,1:T(2,128)S(1)}, f32[96,512]{1,0:T(8,128)S(1)}, s32[]{:T(128)}, /*index=5*/s32[]{:T(128)}) %tuple.38), condition=%wide.while_cond.1, body=%wide.while_body.1.sunk | while | flops 2 | bytes 8305 | solution.py:20
  75.2 1.3 dynamic-slice.15
  77.2 1.3 dynamic-slice.15
  79.3 1.3 dynamic-slice.15
  81.3 1.3 dynamic-slice.15
  83.4 1.3 dynamic-slice.15
  85.5 1.3 dynamic-slice.15
  87.5 1.3 dynamic-slice.15
  89.6 1.3 dynamic-slice.15
  91.6 1.3 dynamic-slice.15
  114.3 1.3 dynamic-slice.15
  116.3 1.3 dynamic-slice.15
  118.4 1.3 dynamic-slice.15
  120.5 1.3 dynamic-slice.15
  122.5 1.3 dynamic-slice.15
  124.6 1.3 dynamic-slice.15
  126.6 1.3 dynamic-slice.15
  128.7 1.3 dynamic-slice.15
  130.7 1.3 dynamic-slice.15
  153.4 1.3 dynamic-slice.15
  155.4 1.3 dynamic-slice.15
  157.5 1.3 dynamic-slice.15
  159.6 1.3 dynamic-slice.15
  161.6 1.3 dynamic-slice.15
  163.7 1.3 dynamic-slice.15
  165.7 1.3 dynamic-slice.15
  167.8 1.3 dynamic-slice.15
  169.9 1.3 dynamic-slice.15
  192.5 1.3 dynamic-slice.15
  194.6 1.3 dynamic-slice.15
  196.6 1.3 dynamic-slice.15
  198.7 1.3 dynamic-slice.15
  200.7 1.3 dynamic-slice.15
  202.8 1.3 dynamic-slice.15
  204.8 1.3 dynamic-slice.15
  206.9 1.3 dynamic-slice.15
  209.0 1.3 dynamic-slice.15
  231.6 1.3 dynamic-slice.15
  233.7 1.3 dynamic-slice.15
  235.7 1.3 dynamic-slice.15
  237.8 1.3 dynamic-slice.15
  239.8 1.3 dynamic-slice.15
  241.9 1.3 dynamic-slice.15
  244.0 1.3 dynamic-slice.15
  246.0 1.3 dynamic-slice.15
  248.1 1.3 dynamic-slice.15
  256.5 28.5 %fusion.1 = f32[1,96,1025]{1,0,2:T(1,128)S(1)} fusion(bf16[1,24,1280]{1,0,2:T(2,128)(2,1)S(1)} %copy.33, s32[96]{0:T(128)S(1)} %copy-done.2, bf16[96,256]{0,1:T(8,128)(2,1)S(1)} %copy.32), kind=kOutput, calls=%fused_computation.4 | convolution fusion | flops 1210318848 | bytes 504576 | tf_op jit(solution)/shard_map/conv_general_dilated | solution.py:30
  285.8 197.6 %while.2 = (s32[]{:T(128)}, f32[96,1024]{1,0:T(8,128)S(1)}, s32[96,2]{0,1:T(2,128)S(1)}, f32[96,512]{1,0:T(8,128)S(1)}, s32[]{:T(128)}, /*index=5*/s32[]{:T(128)}) while((s32[]{:T(128)}, f32[96,1024]{1,0:T(8,128)S(1)}, s32[96,2]{0,1:T(2,128)S(1)}, f32[96,512]{1,0:T(8,128)S(1)}, s32[]{:T(128)}, /*index=5*/s32[]{:T(128)}) %tuple.41), condition=%wide.while_cond, body=%wide.while_body.sunk | while | flops 2 | bytes 8305 | solution.py:20
  307.1 1.3 dynamic-slice.13
  309.2 1.3 dynamic-slice.13
  311.2 1.3 dynamic-slice.13
  313.3 1.3 dynamic-slice.13
  315.3 1.3 dynamic-slice.13
  317.4 1.3 dynamic-slice.13
  319.5 1.3 dynamic-slice.13
  321.5 1.3 dynamic-slice.13
  323.6 1.3 dynamic-slice.13
  346.2 1.3 dynamic-slice.13
  348.3 1.3 dynamic-slice.13
  350.3 1.3 dynamic-slice.13
  352.4 1.3 dynamic-slice.13
  484.1 5.8 %psum.7 = f32[4,512]{1,0:T(4,128)S(1)} all-reduce(f32[4,512]{1,0:T(4,128)S(1)} %fusion.5), channel_id=1, replica_groups=mesh['parts'=2,'tmpl'=4,'sta'=4] {'sta'}, use_global_device_ids=true, to_apply=%region_4.5 | all-reduce | flops 2048 | bytes 16384 | tf_op jit(solution)/shard_map/psum | solution.py:54
  (754 shorter events, 319.7 us)
Async XLA Ops:
  56.7 1.0 copy-start.1
  57.6 198.7 %copy-start = (bf16[8,3,4,256]{3,2,1,0:T(4,128)(2,1)S(1)}, bf16[8,3,4,256]{3,2,1,0:T(4,128)(2,1)}, u32[]{:S(2)}) copy-start(bf16[8,3,4,256]{3,2,1,0:T(4,128)(2,1)} %param.4) | copy-start | bytes 147460
  57.6 198.9 %copy-start.2 = (s32[96]{0:T(128)S(1)}, s32[96]{0:T(128)}, u32[]{:S(2)}) copy-start(s32[96]{0:T(128)} %constant.11.clone.1) | copy-start | bytes 1156
where the time goes:
time: 494 us; the launch traced here: 490 us
  local copies, waits for them, and re-layouts  396 us (80%)
  blocking collectives  53.7 us (11%)
  matrix products  28.5 us (6%)
  other arithmetic  7.52 us (2%)
    gather x768, local copies, waits for them, and re-layouts  391 us
    all_gather x1, blocking collectives, shards(): whole = lax.all_gather(data, 'tmpl', axis=2, tiled=True)  47.9 us
    conv_general_dilated x1, matrix products, local_term(): lax.conv_general_dilated(lowered, kernel, (1,), 'VALID', dimension_number...  28.5 us

commit v1 on v0

--- a/solution.py
+++ b/solution.py
@@ -49,7 +49,12 @@
 
 
 def shards(data, templates, starts):
-    whole = lax.all_gather(data, "tmpl", axis=2, tiled=True)
+    ring = [data]
+    for hop in range(3):
+        ring.append(lax.ppermute(ring[-1], "tmpl", [(dev, (dev + 1) % 4) for dev in range(4)]))
+    whole = jnp.roll(
+        jnp.concatenate(ring[::-1], axis=2), (lax.axis_index("tmpl") + 1) * ring[0].shape[2], axis=2
+    )
     partial_value = local_term(whole, templates, starts)
     summed = lax.psum(partial_value, "sta")
     width = LAGS // lax.axis_size("sta")

time: 494 us -> 464 us (0.939)
  blocking collectives: 53.7 us -> 5.77 us
  waiting for transfers between devices: 0 us -> 12.7 us
    all_gather x1 -> x0, blocking collectives: 47.9 us -> none  [shards(): whole = lax.all_gather(data, 'tmpl', axis=2, tiled=True)]
    ppermute x0 -> x3, waiting for transfers between devices: none -> 12.7 us  [shards(): lax.ppermute(ring[-1], 'tmpl', [(dev, (dev + 1) % 4) for dev in range(4)])]
  transfers between devices with their start and end apart: 0 -> 3, of which waited for: 0 -> 3; matrix products, arithmetic and copies ran while one was open for 0% -> 1% of each run, Pallas kernels for 0% -> 0%
where the time goes in v1:
time: 464 us; the launch traced here: 460 us
  local copies, waits for them, and re-layouts  397 us (86%)
  matrix products  28.5 us (6%)
  waiting for transfers between devices  12.7 us (3%)
  other arithmetic  8.38 us (2%)
  blocking collectives  5.77 us (1%)
  loops' own time  4.65 us (1%)
    gather x768, local copies, waits for them, and re-layouts  391 us
    conv_general_dilated x1, matrix products, local_term(): lax.conv_general_dilated(lowered, kernel, (1,), 'VALID', dimension_number...  28.5 us
    ppermute x3, waiting for transfers between devices, shards(): lax.ppermute(ring[-1], 'tmpl', [(dev, (dev + 1) % 4) for dev in range(4)])  12.7 us
  transfers between devices with their start and end apart: 3, of which 3 were waited for; matrix products, arithmetic and copies ran while one was open for 1% of the time, Pallas kernels for 0%

profile of v1, /device:TPU:0, one launch (start us, length us, event | category | flops | bytes accessed | tf_op | source)
XLA Modules:
  0.0 459.8 jit_solution(16977570191847198459)
XLA Ops:
  0.0 3.0 collective-permute-start
  4.9 2.3 collective-permute-done
  7.2 5.7 %collective-permute-done.1 = f32[8,3,320]{2,0,1:T(8,128)S(1)} collective-permute-done((f32[8,3,320]{2,0,1:T(8,128)S(1)}, f32[8,3,320]{2,0,1:T(8,128)S(1)}, u32[]{:S(2)}, u32[]{:S(2)}) %collective-permute-start.1) | collective-permute-done | bytes 30752 | tf_op jit(solution)/shard_map/ppermute | solution.py:54
  14.1 4.6 %collective-permute-done.2 = f32[8,3,320]{2,0,1:T(8,128)S(1)} collective-permute-done((f32[8,3,320]{2,0,1:T(8,128)S(1)}, f32[8,3,320]{2,0,1:T(8,128)S(1)}, u32[]{:S(2)}, u32[]{:S(2)}) %collective-permute-start.2) | collective-permute-done | bytes 30752 | tf_op jit(solution)/shard_map/ppermute | solution.py:54
  20.1 6.8 %reduce-window.6 = f32[24,10,128]{2,1,0:T(8,128)S(1)} reduce-window(f32[24,10,128]{2,1,0:T(8,128)S(1)} %mul.29, f32[]{:T(128)} %constant.52.clone.1), window={size=1x1x128 pad=0_0x0_0x127_0}, to_apply=%region_1.2 | reduce-window | flops 3901440 | bytes 245764 | tf_op jit(solution)/shard_map/reduce-window
  27.9 197.6 %while.3 = (s32[]{:T(128)}, f32[96,1024]{1,0:T(8,128)S(1)}, s32[96,2]{0,1:T(2,128)S(1)}, f32[96,512]{1,0:T(8,128)S(1)}, s32[]{:T(128)}, /*index=5*/s32[]{:T(128)}) while((s32[]{:T(128)}, f32[96,1024]{1,0:T(8,128)S(1)}, s32[96,2]{0,1:T(2,128)S(1)}, f32[96,512]{1,0:T(8,128)S(1)}, s32[]{:T(128)}, /*index=5*/s32[]{:T(128)}) %tuple.37), condition=%wide.while_cond.1, body=%wide.while_body.1.sunk | while | flops 2 | bytes 8305 | solution.py:20
  28.5 1.3 dynamic-slice.15
  30.6 1.3 dynamic-slice.15
  32.7 1.3 dynamic-slice.15
  34.7 1.3 dynamic-slice.15
  36.8 1.3 dynamic-slice.15
  38.8 1.3 dynamic-slice.15
  40.9 1.3 dynamic-slice.15
  43.0 1.3 dynamic-slice.15
  65.6 1.3 dynamic-slice.15
  67.7 1.3 dynamic-slice.15
  69.7 1.3 dynamic-slice.15
  71.8 1.3 dynamic-slice.15
  73.8 1.3 dynamic-slice.15
  75.9 1.3 dynamic-slice.15
  77.9 1.3 dynamic-slice.15
  80.0 1.3 dynamic-slice.15
  82.1 1.3 dynamic-slice.15
  104.7 1.3 dynamic-slice.15
  106.8 1.3 dynamic-slice.15
  108.8 1.3 dynamic-slice.15
  110.9 1.3 dynamic-slice.15
  112.9 1.3 dynamic-slice.15
  115.0 1.3 dynamic-slice.15
  117.1 1.3 dynamic-slice.15
  119.1 1.3 dynamic-slice.15
  121.2 1.3 dynamic-slice.15
  143.8 1.3 dynamic-slice.15
  145.9 1.3 dynamic-slice.15
  147.9 1.3 dynamic-slice.15
  150.0 1.3 dynamic-slice.15
  152.1 1.3 dynamic-slice.15
  154.1 1.3 dynamic-slice.15
  156.2 1.3 dynamic-slice.15
  158.2 1.3 dynamic-slice.15
  160.3 1.3 dynamic-slice.15
  182.9 1.3 dynamic-slice.15
  185.0 1.3 dynamic-slice.15
  187.0 1.3 dynamic-slice.15
  189.1 1.3 dynamic-slice.15
  191.2 1.3 dynamic-slice.15
  193.2 1.3 dynamic-slice.15
  195.3 1.3 dynamic-slice.15
  197.3 1.3 dynamic-slice.15
  199.4 1.3 dynamic-slice.15
  222.0 1.3 dynamic-slice.15
  224.1 1.3 dynamic-slice.15
  226.2 28.5 %fusion.1 = f32[1,96,1025]{1,0,2:T(1,128)S(1)} fusion(bf16[1,24,1280]{1,0,2:T(2,128)(2,1)S(1)} %copy.30, s32[96]{0:T(128)S(1)} %copy-done, bf16[96,256]{0,1:T(8,128)(2,1)S(1)} %copy.29), kind=kOutput, calls=%fused_computation.4 | convolution fusion | flops 1210318848 | bytes 504576 | tf_op jit(solution)/shard_map/conv_general_dilated | solution.py:30
  255.6 197.6 %while.2 = (s32[]{:T(128)}, f32[96,1024]{1,0:T(8,128)S(1)}, s32[96,2]{0,1:T(2,128)S(1)}, f32[96,512]{1,0:T(8,128)S(1)}, s32[]{:T(128)}, /*index=5*/s32[]{:T(128)}) while((s32[]{:T(128)}, f32[96,1024]{1,0:T(8,128)S(1)}, s32[96,2]{0,1:T(2,128)S(1)}, f32[96,512]{1,0:T(8,128)S(1)}, s32[]{:T(128)}, /*index=5*/s32[]{:T(128)}) %tuple.40), condition=%wide.while_cond, body=%wide.while_body.sunk | while | flops 2 | bytes 8305 | solution.py:20
  272.7 1.3 dynamic-slice.13
  274.8 1.3 dynamic-slice.13
  276.8 1.3 dynamic-slice.13
  278.9 1.3 dynamic-slice.13
  280.9 1.3 dynamic-slice.13
  283.0 1.3 dynamic-slice.13
  285.1 1.3 dynamic-slice.13
  287.1 1.3 dynamic-slice.13
  289.2 1.3 dynamic-slice.13
  453.5 5.8 %psum.7 = f32[4,512]{1,0:T(4,128)S(1)} all-reduce(f32[4,512]{1,0:T(4,128)S(1)} %fusion.5), channel_id=1, replica_groups=mesh['parts'=2,'tmpl'=4,'sta'=4] {'sta'}, use_global_device_ids=true, to_apply=%region_4.5 | all-reduce | flops 2048 | bytes 16384 | tf_op jit(solution)/shard_map/psum | solution.py:59
  (755 shorter events, 325.3 us)
Async XLA Ops:
  0.0 7.2 %collective-permute-start = (f32[8,3,320]{2,0,1:T(8,128)}, f32[8,3,320]{2,0,1:T(8,128)S(1)}, u32[]{:S(2)}, u32[]{:S(2)}) collective-permute-start(f32[8,3,320]{2,0,1:T(8,128)} %param.3), channel_id=1, source_target_pairs={{0,4},{4,8},{8,12},{12,0},{1,5},{5,9},{9,13},{13,1},{2,6},{6,10},{... | collective-permute-start | bytes 92168 | tf_op jit(solution)/shard_map/ppermute | solution.py:54
  7.2 5.8 %collective-permute-start.1 = (f32[8,3,320]{2,0,1:T(8,128)S(1)}, f32[8,3,320]{2,0,1:T(8,128)S(1)}, u32[]{:S(2)}, u32[]{:S(2)}) collective-permute-start(f32[8,3,320]{2,0,1:T(8,128)S(1)} %collective-permute-done), channel_id=1, source_target_pairs={{0,4},{4,8},{8,12},{12,0},{1,5},{5,9},{9,13},{13,1},{2,6},{6,10},{... | collective-permute-start | bytes 92168 | tf_op jit(solution)/shard_map/ppermute | solution.py:54
  13.0 5.8 %collective-permute-start.2 = (f32[8,3,320]{2,0,1:T(8,128)S(1)}, f32[8,3,320]{2,0,1:T(8,128)S(1)}, u32[]{:S(2)}, u32[]{:S(2)}) collective-permute-start(f32[8,3,320]{2,0,1:T(8,128)S(1)} %collective-permute-done.1), channel_id=1, source_target_pairs={{0,4},{4,8},{8,12},{12,0},{1,5},{5,9},{9,13},{13,1},{2,6},{6,10},{... | collective-permute-start | bytes 92168 | tf_op jit(solution)/shard_map/ppermute | solution.py:54
  225.5 0.7 copy-start
